TPU v7x, 32 devices: a whole 2x2x4 slice. The times are simulated.
32 devices in a mesh: inp: 16 (over z, y, core), tm: 2 (over x).
Axes of the slice: x: 2, y: 2, z: 4, core: 2. Of those that a mesh axis runs over, the one named last changes fastest.
Arguments:
- samples: bfloat16 [512, 16384], P('inp', 'tm'), may hold values from -6 to 6
- tail: bfloat16 [512, 6144], P('inp'), may hold values from -6 to 6
- taps: float32 [4, 2048], replicated, may hold values from -3 to 3
- tile_table: int32 [16, 4], P('inp'), may hold values from 0 to 3, as said below
Outputs:
- visibilities: float32 [16, 4, 2, 32, 32, 1024], P('inp', None, None, None, None, 'tm')
Inputs may be any that keep to these rules, and one draw needn't show every extreme that they name: `tile_table`: each row holds 4 distinct offsets; offsets 0 and 3 both occur.
All inputs are finite; a program needn't handle non-finite values.
Results may differ from a plain program's by a relative error of at most 0.0064.
Values may be sent and summed in bfloat16 or wider, within the bound.
A program may use at most 128 MiB of HBM per device.

v0:
```python
import math
import jax
import jax.numpy as jnp
import numpy as np
from jax import lax
from jax.sharding import PartitionSpec as P

F = 1024
L = 2048
TAPS = 4
A_DEV = 32
S_DEV = 4
SPAN = 4


def shifted(array, axis, by):
    peers = lax.axis_size(axis)
    pairs = [(i, i + by) for i in range(peers) if 0 <= i + by < peers]
    return lax.ppermute(array, axis, pairs)


def shifted_2(block, axis, distance):
    devices = range(lax.axis_size(axis))
    route = [((i - distance) % len(devices), i) for i in devices]
    return lax.ppermute(block, axis, route)


def dft_basis():
    sample_rows = np.arange(L, dtype=np.int64)[:, None]
    channel_cols = np.arange(F, dtype=np.int64)[None, :]
    phase_index = sample_rows * channel_cols % L
    table_angles = np.arange(L, dtype=np.float32) * np.float32(2.0 * math.pi / L)
    norm_factor = np.float32(1.0 / math.sqrt(L))
    cosine_table = np.cos(table_angles).astype(np.float32) * norm_factor
    sine_table = -np.sin(table_angles).astype(np.float32) * norm_factor
    whole_table = np.concatenate([cosine_table[phase_index], sine_table[phase_index]], axis=1)
    return jnp.asarray(whole_table, dtype=jnp.bfloat16)


def channelize(frame_stack, count, taps, basis):
    filtered = taps[0][None, None, :] * frame_stack[:, 0:count, :].astype(jnp.float32)
    for tap in range(1, TAPS):
        filtered = filtered + taps[tap][None, None, :] * frame_stack[
            :, tap : tap + count, :
        ].astype(jnp.float32)
    filtered = filtered.astype(jnp.bfloat16).reshape(A_DEV * count, L)
    spectra = jnp.dot(filtered, basis, preferred_element_type=jnp.float32)
    return spectra.astype(jnp.bfloat16).reshape(A_DEV, count, 2, F)


def correlate_all(own_block, partners, spec_count):
    own_major = jnp.transpose(own_block, (3, 0, 2, 1))
    real_own = own_major[:, :, 0, :]
    imag_own = own_major[:, :, 1, :]
    upper_rows = jnp.concatenate([real_own, imag_own], axis=2)
    lower_rows = jnp.concatenate([imag_own, -real_own], axis=2)
    left_stack = jnp.concatenate([upper_rows, lower_rows], axis=1)
    tile_count = partners.shape[0]
    width = partners.shape[1]
    right_stack = jnp.transpose(partners, (4, 3, 2, 0, 1)).reshape(
        partners.shape[4], 2 * spec_count, tile_count * width
    )
    products = lax.dot_general(
        left_stack, right_stack, (((2,), (1,)), ((0,), (0,))), preferred_element_type=jnp.float32
    )
    products = products * (1.0 / spec_count)
    products = products.reshape(partners.shape[4], 2, width, tile_count, width)
    return jnp.transpose(products, (3, 1, 2, 4, 0))


def body(samples, tail, taps, tile_table):
    frames = samples.reshape(A_DEV, S_DEV, L)
    nearby = shifted(frames[:, : TAPS - 1, :], "tm", -1)
    at_end = lax.axis_index("tm") == lax.axis_size("tm") - 1
    trailing = jnp.where(at_end, tail.reshape(A_DEV, TAPS - 1, L), nearby)
    basis = dft_basis()
    complete = jnp.concatenate([frames, trailing], axis=1)
    spectra = channelize(complete, S_DEV, taps, basis)
    turned = lax.all_to_all(spectra, "tm", split_axis=3, concat_axis=1, tiled=True)
    spec_count = turned.shape[1]
    blocks = [turned]
    current = turned
    for section in range(1, SPAN):
        current = shifted_2(current, "inp", -1)
        blocks.append(current)
    holdings = jnp.stack(blocks, axis=0)
    partners = jnp.take(holdings, tile_table[0], axis=0)
    return correlate_all(turned, partners, spec_count)[None]


def solution(mesh):
    in_specs = (P("inp", "tm"), P("inp", None), P(), P("inp", None))
    out_specs = P("inp", None, None, None, None, "tm")
    return jax.shard_map(body, mesh=mesh, in_specs=in_specs, out_specs=out_specs, check_vma=False)
```

profile of v0, /device:TPU:0, one launch (start us, length us, event | category | flops | bytes accessed | tf_op | source)
XLA Modules:
  0.0 127.8 jit_solution(12264836127973082182)
XLA Ops:
  0.0 1.4 %reshape.57 = bf16[32,4,2048]{2,1,0:T(4,128)(2,1)S(1)} reshape(bf16[32,8192]{1,0:T(8,128)(2,1)} %param.5) | data formatting | bytes 1048576 | tf_op jit(solution)/shard_map/reshape | solution.py:72
  1.4 1.3 %collective-permute-start = (bf16[32,3,2048]{2,1,0:T(4,128)(2,1)S(1)}, bf16[32,3,2048]{2,1,0:T(4,128)(2,1)S(1)}, u32[]{:S(2)}, u32[]{:S(2)}) collective-permute-start(bf16[32,3,2048]{2,1,0:T(4,128)(2,1)S(1)} %bitcast.47), channel_id=1, source_target_pairs={{1,0},{3,2},{5,4},{7,6},{9,8},{11,10},{13,12},{15,14},{17,16},{19,... | collective-permute-start | bytes 1179656 | tf_op jit(solution)/shard_map/ppermute | solution.py:19
  2.7 1.7 %reshape.58 = bf16[32,3,2048]{2,1,0:T(4,128)(2,1)S(1)} reshape(bf16[32,6144]{1,0:T(8,128)(2,1)} %param.6) | data formatting | bytes 786432 | tf_op jit(solution)/shard_map/reshape | solution.py:75
  4.4 0.9 fusion.8
  5.4 12.3 %collective-permute-done = bf16[32,3,2048]{2,1,0:T(4,128)(2,1)S(1)} collective-permute-done((bf16[32,3,2048]{2,1,0:T(4,128)(2,1)S(1)}, bf16[32,3,2048]{2,1,0:T(4,128)(2,1)S(1)}, u32[]{:S(2)}, u32[]{:S(2)}) %collective-permute-start) | collective-permute-done | bytes 393248 | tf_op jit(solution)/shard_map/ppermute | solution.py:19
  17.6 0.3 broadcast_select_fusion.1
  17.9 1.8 %add_convert_fusion = bf16[32,4,2048]{2,1,0:T(4,128)(2,1)S(1)} fusion(bf16[32,4,2048]{2,1,0:T(4,128)(2,1)S(1)} %reshape.57, bf16[32,3,2048]{2,1,0:T(4,128)(2,1)S(1)} %broadcast_select_fusion.1, f32[2048]{0:T(1024)S(1)} %bitcast.51, f32[2048]{0:T(1024)S(1)} %bitcast.52, f32[2048]{0:T(1024)S(1)} %bitcast.50, f32[2048]{0:T(1024)S(1)} %bitcast.49), kind=kLoop, calls=%fused_computation.12 | loop fusion | flops 5505024 | bytes 1474560 | tf_op jit(solution)/shard_map/convert_element_type | solution.py:46
  19.8 0.1 reshape.59
  19.9 4.6 %convolution_convert_fusion = bf16[128,2048]{1,0:T(8,128)(2,1)S(1)} fusion(bf16[128,2048]{1,0:T(8,128)(2,1)S(1)} %reshape.59, bf16[2048,2048]{1,0:T(8,128)(2,1)} %constant.26.clone), kind=kOutput, calls=%fused_computation.2 | convolution fusion | flops 1074003968 | bytes 9437184 | tf_op jit(solution)/shard_map/dot_general | solution.py:47
  24.5 0.4 reshape.60
  24.9 1.7 %copy.30 = bf16[32,4,2,1024]{0,1,2,3:T(4,128)(2,1)S(1)} copy(bf16[32,4,2,1024]{3,2,1,0:T(2,128)(2,1)S(1)} %reshape.60) | data formatting | bytes 1048576 | tf_op jit(solution)/shard_map/reshape | solution.py:48
  26.6 2.1 %reshape.71 = bf16[2,2,65536]{2,1,0:T(2,128)(2,1)S(1)} reshape(bf16[1024,2,4,32]{3,2,1,0:T(4,128)(2,1)S(1)} %bitcast.42) | data formatting | bytes 1048576
  28.7 10.1 %all_to_all.18 = bf16[2,2,65536]{2,1,0:T(2,128)(2,1)S(1)} all-to-all(bf16[2,2,65536]{2,1,0:T(2,128)(2,1)S(1)} %reshape.71), channel_id=1, replica_groups=mesh['inp'=16,'tm'=2] {'tm'}, dimensions={0} | all-to-all | bytes 1048576 | tf_op jit(solution)/shard_map/all_to_all | solution.py:79
  38.8 1.0 reshape.72
  39.9 1.9 %copy.31 = bf16[32,2,4,2,512]{4,2,1,3,0:T(4,128)(2,1)S(1)} copy(bf16[32,2,4,2,512]{0,2,3,4,1:T(4,128)(2,1)S(1)} %bitcast.43) | data formatting | bytes 1048576 | tf_op jit(solution)/shard_map/all_to_all | solution.py:79
  41.8 0.1 all_to_all.16
  41.9 2.8 %collective-permute-start.1 = (bf16[32,8,2,512]{3,1,2,0:T(8,128)(2,1)S(1)}, bf16[32,8,2,512]{3,1,2,0:T(8,128)(2,1)S(1)}, u32[]{:S(2)}, u32[]{:S(2)}) collective-permute-start(bf16[32,8,2,512]{3,1,2,0:T(8,128)(2,1)S(1)} %all_to_all.16), channel_id=1, source_target_pairs={{2,0},{4,2},{6,4},{8,6},{10,8},{12,10},{14,12},{16,14},{18,16},{20... | collective-permute-start | bytes 1572872 | tf_op jit(solution)/shard_map/ppermute | solution.py:25
  44.7 6.7 %collective-permute-done.1 = bf16[32,8,2,512]{3,1,2,0:T(8,128)(2,1)S(1)} collective-permute-done((bf16[32,8,2,512]{3,1,2,0:T(8,128)(2,1)S(1)}, bf16[32,8,2,512]{3,1,2,0:T(8,128)(2,1)S(1)}, u32[]{:S(2)}, u32[]{:S(2)}) %collective-permute-start.1) | collective-permute-done | bytes 524320 | tf_op jit(solution)/shard_map/ppermute | solution.py:25
  51.4 4.6 %collective-permute-start.2 = (bf16[32,8,2,512]{3,1,2,0:T(8,128)(2,1)S(1)}, bf16[32,8,2,512]{3,1,2,0:T(8,128)(2,1)}, u32[]{:S(2)}, u32[]{:S(2)}) collective-permute-start(bf16[32,8,2,512]{3,1,2,0:T(8,128)(2,1)S(1)} %collective-permute-done.1), channel_id=1, source_target_pairs={{2,0},{4,2},{6,4},{8,6},{10,8},{12,10},{14,12},{16,14},{18,16},{20... | collective-permute-start | bytes 1572872 | tf_op jit(solution)/shard_map/ppermute | solution.py:25
  56.1 0.1 stack.15
  56.2 6.5 %collective-permute-done.2 = bf16[32,8,2,512]{3,1,2,0:T(8,128)(2,1)} collective-permute-done((bf16[32,8,2,512]{3,1,2,0:T(8,128)(2,1)S(1)}, bf16[32,8,2,512]{3,1,2,0:T(8,128)(2,1)}, u32[]{:S(2)}, u32[]{:S(2)}) %collective-permute-start.2) | collective-permute-done | bytes 524320 | tf_op jit(solution)/shard_map/ppermute | solution.py:25
  62.8 4.7 %collective-permute-start.3 = (bf16[32,8,2,512]{3,1,2,0:T(8,128)(2,1)}, bf16[32,8,2,512]{3,1,2,0:T(8,128)(2,1)}, u32[]{:S(2)}, u32[]{:S(2)}) collective-permute-start(bf16[32,8,2,512]{3,1,2,0:T(8,128)(2,1)} %collective-permute-done.2), channel_id=1, source_target_pairs={{2,0},{4,2},{6,4},{8,6},{10,8},{12,10},{14,12},{16,14},{18,16},{20... | collective-permute-start | bytes 1572872 | tf_op jit(solution)/shard_map/ppermute | solution.py:25
  67.7 3.0 %copy.32 = bf16[512,32,16]{1,2,0:T(8,128)(2,1)} copy(bf16[512,32,16]{0,2,1:T(8,128)(2,1)S(1)} %get-tuple-element.7) | data formatting | bytes 1048576 | tf_op jit(solution)/shard_map/concatenate | solution.py:55
  70.7 3.1 %copy.33 = bf16[512,32,16]{1,2,0:T(8,128)(2,1)} copy(bf16[512,32,16]{0,2,1:T(8,128)(2,1)S(1)} %get-tuple-element.8) | data formatting | bytes 1048576 | tf_op jit(solution)/shard_map/concatenate | solution.py:56
  73.8 0.7 collective-permute-done.3
  74.5 1.5 %pad_maximum_fusion = bf16[4,32,8,2,512]{4,2,3,1,0:T(8,128)(2,1)S(1)} fusion(bf16[1,32,8,2,512]{4,2,3,1,0:T(8,128)(2,1)} %bitcast.13, bf16[1,32,8,2,512]{4,2,3,1,0:T(8,128)(2,1)} %bitcast.12, bf16[1,32,8,2,512]{4,2,3,1,0:T(8,128)(2,1)S(1)} %bitcast.48, bf16[1,32,8,2,512]{4,2,3,1,0:T(8,128)(2,1)S(1)} %stack.15), kind=kLoop, calls=%fused_computation.6 | loop fusion | flops 3145728 | bytes 4194304 | tf_op jit(solution)/shard_map/stack | solution.py:86
  75.9 2.0 %gather_fusion = bf16[4,32,8,2,512]{4,2,3,1,0:T(8,128)(2,1)} fusion(bf16[4,32,8,2,512]{4,2,3,1,0:T(8,128)(2,1)S(1)} %pad_maximum_fusion, s32[1024]{0:T(1024)S(1)} %pad_clamp_fusion), kind=kCustom, calls=%fused_computation | custom fusion | bytes 4194320 | tf_op jit(solution)/shard_map/jit(_take)/gather | solution.py:87
  77.9 1.9 %broadcast_select_fusion = bf16[4,32,8,2,512]{4,2,3,1,0:T(8,128)(2,1)S(1)} fusion(bf16[4,32,8,2,512]{4,2,3,1,0:T(8,128)(2,1)} %gather_fusion, pred[4]{0:T(512)(128)(4,1)S(1)} %compare_and_fusion), kind=kLoop, calls=%fused_computation.7 | loop fusion | flops 1048576 | bytes 4194308 | tf_op jit(solution)/shard_map/jit(_take)/select_n | solution.py:87
  79.8 3.9 %copy.36 = bf16[512,16,128]{2,1,0:T(8,128)(2,1)} copy(bf16[512,16,128]{0,1,2:T(8,128)(2,1)S(1)} %bitcast.44) | data formatting | bytes 4194304 | tf_op jit(solution)/shard_map/reshape | solution.py:60
  83.7 14.2 %convolution_multiply_fusion = f32[512,64,128]{2,1,0:T(8,128)} fusion(bf16[512,16,128]{2,1,0:T(8,128)(2,1)} %copy.36, bf16[512,32,16]{1,2,0:T(8,128)(2,1)} %copy.33, bf16[512,32,16]{1,2,0:T(8,128)(2,1)} %copy.32), kind=kOutput, calls=%fused_computation.1 | convolution fusion | flops 140509184 | bytes 19922944 | tf_op jit(solution)/shard_map/dot_general | solution.py:63
  97.9 17.5 %copy.37 = f32[512,64,128]{0,2,1:T(8,128)} copy(f32[512,64,128]{2,1,0:T(8,128)} %convolution_multiply_fusion) | data formatting | bytes 33554432 | tf_op jit(solution)/shard_map/mul | solution.py:66
  115.4 12.4 %copy.38 = f32[1,4,2,32,32,512]{5,4,3,2,1,0:T(8,128)} copy(f32[1,4,2,32,32,512]{5,4,1,3,2,0:T(8,128)} %bitcast.41) | data formatting | bytes 33554432 | tf_op jit(solution)/shard_map/broadcast_in_dim | solution.py:88
  (12 shorter events, 0.2 us)
Async XLA Ops:
  1.4 16.2 %collective-permute-start = (bf16[32,3,2048]{2,1,0:T(4,128)(2,1)S(1)}, bf16[32,3,2048]{2,1,0:T(4,128)(2,1)S(1)}, u32[]{:S(2)}, u32[]{:S(2)}) collective-permute-start(bf16[32,3,2048]{2,1,0:T(4,128)(2,1)S(1)} %bitcast.47), channel_id=1, source_target_pairs={{1,0},{3,2},{5,4},{7,6},{9,8},{11,10},{13,12},{15,14},{17,16},{19,... | collective-permute-start | bytes 1179656 | tf_op jit(solution)/shard_map/ppermute | solution.py:19
  39.8 16.2 %copy-start.2 = (s32[1,4]{1,0:T(1,128)S(1)}, s32[1,4]{1,0:T(1,128)}, u32[]{:S(2)}) copy-start(s32[1,4]{1,0:T(1,128)} %param.8) | copy-start | bytes 52
  41.9 9.5 %collective-permute-start.1 = (bf16[32,8,2,512]{3,1,2,0:T(8,128)(2,1)S(1)}, bf16[32,8,2,512]{3,1,2,0:T(8,128)(2,1)S(1)}, u32[]{:S(2)}, u32[]{:S(2)}) collective-permute-start(bf16[32,8,2,512]{3,1,2,0:T(8,128)(2,1)S(1)} %all_to_all.16), channel_id=1, source_target_pairs={{2,0},{4,2},{6,4},{8,6},{10,8},{12,10},{14,12},{16,14},{18,16},{20... | collective-permute-start | bytes 1572872 | tf_op jit(solution)/shard_map/ppermute | solution.py:25
  51.4 16.1 %copy-start = (bf16[32,8,2,512]{3,1,2,0:T(8,128)(2,1)}, bf16[32,8,2,512]{3,1,2,0:T(8,128)(2,1)S(1)}, u32[]{:S(2)}) copy-start(bf16[32,8,2,512]{3,1,2,0:T(8,128)(2,1)S(1)} %collective-permute-done.1) | copy-start | bytes 1572868
  51.4 11.3 %collective-permute-start.2 = (bf16[32,8,2,512]{3,1,2,0:T(8,128)(2,1)S(1)}, bf16[32,8,2,512]{3,1,2,0:T(8,128)(2,1)}, u32[]{:S(2)}, u32[]{:S(2)}) collective-permute-start(bf16[32,8,2,512]{3,1,2,0:T(8,128)(2,1)S(1)} %collective-permute-done.1), channel_id=1, source_target_pairs={{2,0},{4,2},{6,4},{8,6},{10,8},{12,10},{14,12},{16,14},{18,16},{20... | collective-permute-start | bytes 1572872 | tf_op jit(solution)/shard_map/ppermute | solution.py:25
  62.8 11.7 %collective-permute-start.3 = (bf16[32,8,2,512]{3,1,2,0:T(8,128)(2,1)}, bf16[32,8,2,512]{3,1,2,0:T(8,128)(2,1)}, u32[]{:S(2)}, u32[]{:S(2)}) collective-permute-start(bf16[32,8,2,512]{3,1,2,0:T(8,128)(2,1)} %collective-permute-done.2), channel_id=1, source_target_pairs={{2,0},{4,2},{6,4},{8,6},{10,8},{12,10},{14,12},{16,14},{18,16},{20... | collective-permute-start | bytes 1572872 | tf_op jit(solution)/shard_map/ppermute | solution.py:25
  67.6 6.8 %copy-start.1 = (bf16[32,8,2,512]{3,1,2,0:T(8,128)(2,1)S(1)}, bf16[32,8,2,512]{3,1,2,0:T(8,128)(2,1)}, u32[]{:S(2)}) copy-start(bf16[32,8,2,512]{3,1,2,0:T(8,128)(2,1)} %copy-done) | copy-start | bytes 1572868
where the time goes:
time: 128 us
  local copies, waits for them, and re-layouts  53.4 us (42%)
  waiting for transfers between devices  26.3 us (21%)
  matrix products  18.8 us (15%)
  starting transfers between devices  13.4 us (10%)
  blocking collectives  10.1 us (8%)
  other arithmetic  5.56 us (4%)
    mul x1, local copies, waits for them, and re-layouts, correlate_all(): products = products * (1.0 / spec_count)  17.5 us
    dot_general x1, matrix products, correlate_all(): lax.dot_general(left_stack, right_stack, (((2,), (1,)), ((0,), (0,))), pr...  14.2 us
    ppermute x3, waiting for transfers between devices, shifted_2(): return lax.ppermute(block, axis, route)  14 us
    broadcast_in_dim x1, local copies, waits for them, and re-layouts, body(): return correlate_all(turned, partners, spec_count)[None]  12.4 us
    ppermute x1, waiting for transfers between devices, shifted(): return lax.ppermute(array, axis, pairs)  12.3 us
    ppermute x3, starting transfers between devices, shifted_2(): return lax.ppermute(block, axis, route)  12.1 us
    all_to_all x1, blocking collectives, body(): lax.all_to_all(spectra, 'tm', split_axis=3, concat_axis=1, tiled=True)  10.1 us
    dot_general x1, matrix products, channelize(): spectra = jnp.dot(filtered, basis, preferred_element_type=jnp.float32)  4.64 us
  transfers between devices with their start and end apart: 4, of which 4 were waited for; matrix products, arithmetic and copies ran while one was open for 7% of the time, Pallas kernels for 0%

commit v1 on v0

--- a/solution.py
+++ b/solution.py
@@ -76,7 +76,10 @@
     basis = dft_basis()
     complete = jnp.concatenate([frames, trailing], axis=1)
     spectra = channelize(complete, S_DEV, taps, basis)
-    turned = lax.all_to_all(spectra, "tm", split_axis=3, concat_axis=1, tiled=True)
+    turned = jnp.concatenate(
+        lax.all_to_all(jnp.stack(jnp.split(spectra, lax.axis_size("tm"), axis=3)), "tm", 0, 0),
+        axis=1,
+    )
     spec_count = turned.shape[1]
     blocks = [turned]
     current = turned

time: 128 us -> 123 us (0.961)
  local copies, waits for them, and re-layouts: 53.4 us -> 47.4 us
    unnamed x8 -> x2, local copies, waits for them, and re-layouts: 3.11 us -> 0.01 us
    all_to_all x2 -> x0, local copies, waits for them, and re-layouts: 2.06 us -> none  [body(): lax.all_to_all(spectra, 'tm', split_axis=3, concat_axis=1, tiled=True)]
    reshape x2 -> x1, local copies, waits for them, and re-layouts: 2.04 us -> 0.38 us  [channelize(): return spectra.astype(jnp.bfloat16).reshape(A_DEV, count, 2, F)]
where the time goes in v1:
time: 123 us; the launch traced here: 122 us
  local copies, waits for them, and re-layouts  47.4 us (39%)
  waiting for transfers between devices  26.3 us (21%)
  matrix products  18.8 us (15%)
  starting transfers between devices  13.4 us (11%)
  blocking collectives  10.1 us (8%)
  other arithmetic  6.29 us (5%)
    mul x1, local copies, waits for them, and re-layouts, correlate_all(): products = products * (1.0 / spec_count)  17.5 us
    dot_general x1, matrix products, correlate_all(): lax.dot_general(left_stack, right_stack, (((2,), (1,)), ((0,), (0,))), pr...  14.2 us
    ppermute x3, waiting for transfers between devices, shifted_2(): return lax.ppermute(block, axis, route)  14 us
    broadcast_in_dim x1, local copies, waits for them, and re-layouts, body(): return correlate_all(turned, partners, spec_count)[None]  12.4 us
    ppermute x1, waiting for transfers between devices, shifted(): return lax.ppermute(array, axis, pairs)  12.3 us
    ppermute x3, starting transfers between devices, shifted_2(): return lax.ppermute(block, axis, route)  12.1 us
    all_to_all x1, blocking collectives, body(): lax.all_to_all(jnp.stack(jnp.split(spectra, lax.axis_size('tm'), axis=3))...  10.1 us
    dot_general x1, matrix products, channelize(): spectra = jnp.dot(filtered, basis, preferred_element_type=jnp.float32)  4.64 us
  transfers between devices with their start and end apart: 4, of which 4 were waited for; matrix products, arithmetic and copies ran while one was open for 7% of the time, Pallas kernels for 0%

profile of v1, /device:TPU:0, one launch (start us, length us, event | category | flops | bytes accessed | tf_op | source)
XLA Modules:
  0.0 122.5 jit_solution(17000344314586371005)
XLA Ops:
  0.0 1.4 %reshape.62 = bf16[32,4,2048]{2,1,0:T(4,128)(2,1)S(1)} reshape(bf16[32,8192]{1,0:T(8,128)(2,1)} %param.5) | data formatting | bytes 1048576 | tf_op jit(solution)/shard_map/reshape | solution.py:72
  1.4 1.3 %collective-permute-start = (bf16[32,3,2048]{2,1,0:T(4,128)(2,1)S(1)}, bf16[32,3,2048]{2,1,0:T(4,128)(2,1)S(1)}, u32[]{:S(2)}, u32[]{:S(2)}) collective-permute-start(bf16[32,3,2048]{2,1,0:T(4,128)(2,1)S(1)} %bitcast.45), channel_id=1, source_target_pairs={{1,0},{3,2},{5,4},{7,6},{9,8},{11,10},{13,12},{15,14},{17,16},{19,... | collective-permute-start | bytes 1179656 | tf_op jit(solution)/shard_map/ppermute | solution.py:19
  2.7 1.7 %reshape.63 = bf16[32,3,2048]{2,1,0:T(4,128)(2,1)S(1)} reshape(bf16[32,6144]{1,0:T(8,128)(2,1)} %param.6) | data formatting | bytes 786432 | tf_op jit(solution)/shard_map/reshape | solution.py:75
  4.4 0.9 fusion.8
  5.4 12.3 %collective-permute-done = bf16[32,3,2048]{2,1,0:T(4,128)(2,1)S(1)} collective-permute-done((bf16[32,3,2048]{2,1,0:T(4,128)(2,1)S(1)}, bf16[32,3,2048]{2,1,0:T(4,128)(2,1)S(1)}, u32[]{:S(2)}, u32[]{:S(2)}) %collective-permute-start) | collective-permute-done | bytes 393248 | tf_op jit(solution)/shard_map/ppermute | solution.py:19
  17.6 0.3 broadcast_select_fusion.1
  17.9 1.8 %add_convert_fusion = bf16[32,4,2048]{2,1,0:T(4,128)(2,1)S(1)} fusion(bf16[32,4,2048]{2,1,0:T(4,128)(2,1)S(1)} %reshape.62, bf16[32,3,2048]{2,1,0:T(4,128)(2,1)S(1)} %broadcast_select_fusion.1, f32[2048]{0:T(1024)S(1)} %bitcast.50, f32[2048]{0:T(1024)S(1)} %bitcast.51, f32[2048]{0:T(1024)S(1)} %bitcast.49, f32[2048]{0:T(1024)S(1)} %bitcast.48), kind=kLoop, calls=%fused_computation.12 | loop fusion | flops 5505024 | bytes 1474560 | tf_op jit(solution)/shard_map/convert_element_type | solution.py:46
  19.8 0.1 reshape.64
  19.9 4.6 %convolution_convert_fusion = bf16[128,2048]{1,0:T(8,128)(2,1)S(1)} fusion(bf16[128,2048]{1,0:T(8,128)(2,1)S(1)} %reshape.64, bf16[2048,2048]{1,0:T(8,128)(2,1)} %constant.26.clone), kind=kOutput, calls=%fused_computation.2 | convolution fusion | flops 1074003968 | bytes 9437184 | tf_op jit(solution)/shard_map/dot_general | solution.py:47
  24.5 0.4 reshape.65
  24.9 0.4 slice_bitcast_fusion.3
  25.3 0.7 pad_maximum_fusion.2
  26.0 10.1 %all_to_all.5 = bf16[2,32,4,2,512]{4,3,2,1,0:T(2,128)(2,1)S(1)} all-to-all(bf16[2,32,4,2,512]{4,3,2,1,0:T(2,128)(2,1)S(1)} %pad_maximum_fusion.2), channel_id=1, replica_groups=mesh['inp'=16,'tm'=2] {'tm'}, dimensions={0} | all-to-all | bytes 1048576 | tf_op jit(solution)/shard_map/all_to_all | solution.py:80
  36.2 0.3 copy.22
  36.5 0.1 reshape.67
  36.6 2.8 %collective-permute-start.1 = (bf16[32,8,2,512]{3,1,2,0:T(8,128)(2,1)S(1)}, bf16[32,8,2,512]{3,1,2,0:T(8,128)(2,1)S(1)}, u32[]{:S(2)}, u32[]{:S(2)}) collective-permute-start(bf16[32,8,2,512]{3,1,2,0:T(8,128)(2,1)S(1)} %reshape.67), channel_id=1, source_target_pairs={{2,0},{4,2},{6,4},{8,6},{10,8},{12,10},{14,12},{16,14},{18,16},{20... | collective-permute-start | bytes 1572872 | tf_op jit(solution)/shard_map/ppermute | solution.py:25
  39.4 6.7 %collective-permute-done.1 = bf16[32,8,2,512]{3,1,2,0:T(8,128)(2,1)S(1)} collective-permute-done((bf16[32,8,2,512]{3,1,2,0:T(8,128)(2,1)S(1)}, bf16[32,8,2,512]{3,1,2,0:T(8,128)(2,1)S(1)}, u32[]{:S(2)}, u32[]{:S(2)}) %collective-permute-start.1) | collective-permute-done | bytes 524320 | tf_op jit(solution)/shard_map/ppermute | solution.py:25
  46.1 4.6 %collective-permute-start.2 = (bf16[32,8,2,512]{3,1,2,0:T(8,128)(2,1)S(1)}, bf16[32,8,2,512]{3,1,2,0:T(8,128)(2,1)}, u32[]{:S(2)}, u32[]{:S(2)}) collective-permute-start(bf16[32,8,2,512]{3,1,2,0:T(8,128)(2,1)S(1)} %collective-permute-done.1), channel_id=1, source_target_pairs={{2,0},{4,2},{6,4},{8,6},{10,8},{12,10},{14,12},{16,14},{18,16},{20... | collective-permute-start | bytes 1572872 | tf_op jit(solution)/shard_map/ppermute | solution.py:25
  50.8 0.1 stack_reshape.3
  50.9 6.5 %collective-permute-done.2 = bf16[32,8,2,512]{3,1,2,0:T(8,128)(2,1)} collective-permute-done((bf16[32,8,2,512]{3,1,2,0:T(8,128)(2,1)S(1)}, bf16[32,8,2,512]{3,1,2,0:T(8,128)(2,1)}, u32[]{:S(2)}, u32[]{:S(2)}) %collective-permute-start.2) | collective-permute-done | bytes 524320 | tf_op jit(solution)/shard_map/ppermute | solution.py:25
  57.4 4.7 %collective-permute-start.3 = (bf16[32,8,2,512]{3,1,2,0:T(8,128)(2,1)}, bf16[32,8,2,512]{3,1,2,0:T(8,128)(2,1)}, u32[]{:S(2)}, u32[]{:S(2)}) collective-permute-start(bf16[32,8,2,512]{3,1,2,0:T(8,128)(2,1)} %collective-permute-done.2), channel_id=1, source_target_pairs={{2,0},{4,2},{6,4},{8,6},{10,8},{12,10},{14,12},{16,14},{18,16},{20... | collective-permute-start | bytes 1572872 | tf_op jit(solution)/shard_map/ppermute | solution.py:25
  62.2 0.1 pad_maximum_fusion.3
  62.3 3.0 %copy.23 = bf16[512,32,16]{1,2,0:T(8,128)(2,1)} copy(bf16[512,32,16]{0,2,1:T(8,128)(2,1)S(1)} %get-tuple-element.9) | data formatting | bytes 1048576 | tf_op jit(solution)/shard_map/concatenate | solution.py:55
  65.3 3.1 %copy.24 = bf16[512,32,16]{1,2,0:T(8,128)(2,1)} copy(bf16[512,32,16]{0,2,1:T(8,128)(2,1)S(1)} %get-tuple-element.10) | data formatting | bytes 1048576 | tf_op jit(solution)/shard_map/concatenate | solution.py:56
  68.4 0.8 collective-permute-done.3
  69.2 1.5 %pad_maximum_fusion = bf16[4,32,8,2,512]{4,2,3,1,0:T(8,128)(2,1)S(1)} fusion(bf16[1,32,8,2,512]{4,2,3,1,0:T(8,128)(2,1)} %bitcast.13, bf16[1,32,8,2,512]{4,2,3,1,0:T(8,128)(2,1)} %bitcast.12, bf16[1,32,8,2,512]{4,2,3,1,0:T(8,128)(2,1)S(1)} %bitcast.47, bf16[1,32,8,2,512]{4,2,3,1,0:T(8,128)(2,1)S(1)} %stack_reshape.3), kind=kLoop, calls=%fused_computation.6 | loop fusion | flops 3145728 | bytes 4194304 | tf_op jit(solution)/shard_map/stack | solution.py:89
  70.6 2.0 %gather_fusion = bf16[4,32,8,2,512]{4,2,3,1,0:T(8,128)(2,1)} fusion(bf16[4,32,8,2,512]{4,2,3,1,0:T(8,128)(2,1)S(1)} %pad_maximum_fusion, s32[1024]{0:T(1024)S(1)} %pad_clamp_fusion), kind=kCustom, calls=%fused_computation | custom fusion | bytes 4194320 | tf_op jit(solution)/shard_map/jit(_take)/gather | solution.py:90
  72.6 1.9 %broadcast_select_fusion = bf16[4,32,8,2,512]{4,2,3,1,0:T(8,128)(2,1)S(1)} fusion(bf16[4,32,8,2,512]{4,2,3,1,0:T(8,128)(2,1)} %gather_fusion, pred[4]{0:T(512)(128)(4,1)S(1)} %compare_and_fusion), kind=kLoop, calls=%fused_computation.7 | loop fusion | flops 1048576 | bytes 4194308 | tf_op jit(solution)/shard_map/jit(_take)/select_n | solution.py:90
  74.5 3.9 %copy.27 = bf16[512,16,128]{2,1,0:T(8,128)(2,1)} copy(bf16[512,16,128]{0,1,2:T(8,128)(2,1)S(1)} %bitcast.42) | data formatting | bytes 4194304 | tf_op jit(solution)/shard_map/reshape | solution.py:60
  78.4 14.2 %convolution_multiply_fusion = f32[512,64,128]{2,1,0:T(8,128)} fusion(bf16[512,16,128]{2,1,0:T(8,128)(2,1)} %copy.27, bf16[512,32,16]{1,2,0:T(8,128)(2,1)} %copy.24, bf16[512,32,16]{1,2,0:T(8,128)(2,1)} %copy.23), kind=kOutput, calls=%fused_computation.1 | convolution fusion | flops 140509184 | bytes 19922944 | tf_op jit(solution)/shard_map/dot_general | solution.py:63
  92.6 17.5 %copy.28 = f32[512,64,128]{0,2,1:T(8,128)} copy(f32[512,64,128]{2,1,0:T(8,128)} %convolution_multiply_fusion) | data formatting | bytes 33554432 | tf_op jit(solution)/shard_map/mul | solution.py:66
  110.1 12.4 %copy.29 = f32[1,4,2,32,32,512]{5,4,3,2,1,0:T(8,128)} copy(f32[1,4,2,32,32,512]{5,4,1,3,2,0:T(8,128)} %bitcast.41) | data formatting | bytes 33554432 | tf_op jit(solution)/shard_map/broadcast_in_dim | solution.py:91
  (7 shorter events, 0.1 us)
Async XLA Ops:
  1.4 16.2 %collective-permute-start = (bf16[32,3,2048]{2,1,0:T(4,128)(2,1)S(1)}, bf16[32,3,2048]{2,1,0:T(4,128)(2,1)S(1)}, u32[]{:S(2)}, u32[]{:S(2)}) collective-permute-start(bf16[32,3,2048]{2,1,0:T(4,128)(2,1)S(1)} %bitcast.45), channel_id=1, source_target_pairs={{1,0},{3,2},{5,4},{7,6},{9,8},{11,10},{13,12},{15,14},{17,16},{19,... | collective-permute-start | bytes 1179656 | tf_op jit(solution)/shard_map/ppermute | solution.py:19
  25.3 25.4 %copy-start = (s32[1,4]{1,0:T(1,128)S(1)}, s32[1,4]{1,0:T(1,128)}, u32[]{:S(2)}) copy-start(s32[1,4]{1,0:T(1,128)} %param.8) | copy-start | bytes 52
  36.6 9.5 %collective-permute-start.1 = (bf16[32,8,2,512]{3,1,2,0:T(8,128)(2,1)S(1)}, bf16[32,8,2,512]{3,1,2,0:T(8,128)(2,1)S(1)}, u32[]{:S(2)}, u32[]{:S(2)}) collective-permute-start(bf16[32,8,2,512]{3,1,2,0:T(8,128)(2,1)S(1)} %reshape.67), channel_id=1, source_target_pairs={{2,0},{4,2},{6,4},{8,6},{10,8},{12,10},{14,12},{16,14},{18,16},{20... | collective-permute-start | bytes 1572872 | tf_op jit(solution)/shard_map/ppermute | solution.py:25
  46.1 11.3 %collective-permute-start.2 = (bf16[32,8,2,512]{3,1,2,0:T(8,128)(2,1)S(1)}, bf16[32,8,2,512]{3,1,2,0:T(8,128)(2,1)}, u32[]{:S(2)}, u32[]{:S(2)}) collective-permute-start(bf16[32,8,2,512]{3,1,2,0:T(8,128)(2,1)S(1)} %collective-permute-done.1), channel_id=1, source_target_pairs={{2,0},{4,2},{6,4},{8,6},{10,8},{12,10},{14,12},{16,14},{18,16},{20... | collective-permute-start | bytes 1572872 | tf_op jit(solution)/shard_map/ppermute | solution.py:25
  57.4 11.7 %collective-permute-start.3 = (bf16[32,8,2,512]{3,1,2,0:T(8,128)(2,1)}, bf16[32,8,2,512]{3,1,2,0:T(8,128)(2,1)}, u32[]{:S(2)}, u32[]{:S(2)}) collective-permute-start(bf16[32,8,2,512]{3,1,2,0:T(8,128)(2,1)} %collective-permute-done.2), channel_id=1, source_target_pairs={{2,0},{4,2},{6,4},{8,6},{10,8},{12,10},{14,12},{16,14},{18,16},{20... | collective-permute-start | bytes 1572872 | tf_op jit(solution)/shard_map/ppermute | solution.py:25
